TPU v7x, 128 devices: a whole 4x4x4 slice. The times are simulated.
128 devices in a mesh: stream: 8 (over x, z_lo), span: 16 (over y, z_hi, core).
Axes of the slice: x: 4, y: 4, z: 4 (z_hi: 2, z_lo: 2; z = z_hi * 2 + z_lo), core: 2. Of those that a mesh axis runs over, the one named last changes fastest.
Arguments:
- right_side: float32 [4, 262144], P(None, ('stream', 'span')), may hold values from -5 to 6
- fine_values: float32 [8, 4, 4, 262144], P(None, None, None, ('stream', 'span')), as said below
- fine_columns: int32 [8, 262144], P(None, ('stream', 'span')), may hold values from 0 to 2303, as said below
- fine_sends: int32 [4, 8192], P(None, ('stream', 'span')), may hold values from 0 to 2047, as said below
- fine_order: int32 [128, 2048], P(('stream', 'span')), may hold values from 0 to 2047, each once within a row
- fine_weights: float32 [4, 4, 262144], P(None, None, ('stream', 'span')), may hold values from -0.6 to 1.2
- middle_values: float32 [8, 4, 4, 65536], P(None, None, None, ('stream', 'span')), as said below
- middle_columns: int32 [8, 65536], P(None, ('stream', 'span')), may hold values from 0 to 767, as said below
- middle_sends: int32 [4, 8192], P(None, ('stream', 'span')), may hold values from 0 to 511, as said below
- middle_order: int32 [128, 512], P(('stream', 'span')), may hold values from 0 to 511, each once within a row
- middle_weights: float32 [4, 4, 65536], P(None, None, ('stream', 'span')), may hold values from -0.6 to 1.2
- coarsest_values: float32 [8, 4, 4, 16384], P(None, None, None, ('stream', 'span')), as said below
- coarsest_columns: int32 [8, 16384], P(None, ('stream', 'span')), may hold values from 0 to 2047, as said below
Outputs:
- solution: float32 [4, 262144], P(None, ('stream', 'span'))
- residual: float32 [4, 262144], P(None, ('stream', 'span'))
Inputs may be any that keep to these rules, and one draw needn't show every extreme that they name: `fine_sends`: entry [d, p * 64 + s] is a local row block of device p sent in direction d (0: lower stream index, 1: higher stream index, 2: lower span index, 3: higher span index). Each list has a length of at most 64, which differs between devices and directions and is 64 on some device; rows may repeat within a list, and the slots at or after the length repeat the list's slot 0 as padding. `middle_sends`: as for the first level, with local row blocks of the second level. `fine_columns`: block k = 0 of row block n names its own local row. Entries below 2048 are local row blocks; an entry 2048 + e * 64 + s names slot s of halo block e. Where halo block e has a sending device, s is below the length of that device's list; where it has none (the block is zero), s may be any slot below 64. `middle_columns`: as for the first level with 512 local row blocks. `coarsest_columns`: block k = 0 names the row block itself within its slab; the others name row blocks of the same slab. `fine_values`: each diagonal entry of the k = 0 block is 1 or more, and the other 31 entries of its row over all 8 blocks have absolute values summing to at most 0.9 times it. `middle_values`: as for the first level. `coarsest_values`: as for the first level.
All inputs are finite; a program needn't handle non-finite values.
Results may differ from a plain program's by a relative error of at most 0.0003.
Values sent between devices are 32-bit elements; how exact they have to be, the bound alone decides.
A program may use at most 64 MiB of HBM per device.

v0:
```python
import math

import jax
import jax.numpy as jnp
from jax import lax
from jax.sharding import PartitionSpec as P

KSM = 3
KC = 4


CHEB_CENTRE = 1.0
CHEB_RADIUS = 0.9


def padded(cells, sides, width, closed):
    for axis, dim in sides:
        count = lax.axis_size(axis)
        ends = count if closed else count - 1
        head = lax.slice_in_dim(cells, 0, width, axis=dim)
        tail = lax.slice_in_dim(cells, cells.shape[dim] - width, cells.shape[dim], axis=dim)
        cells = jnp.concatenate(
            [
                lax.ppermute(tail, axis, [(i, (i + 1) % count) for i in range(ends)]),
                cells,
                lax.ppermute(head, axis, [((i + 1) % count, i) for i in range(ends)]),
            ],
            axis=dim,
        )
    return cells


def chebyshev(operate, inverse_diag, target, initial, degree):
    sigma_value = CHEB_CENTRE / CHEB_RADIUS
    rho_prev = 1.0 / sigma_value
    if initial is None:
        iterate = jnp.zeros_like(target)
        current = target
    else:
        iterate = initial
        current = target - operate(initial)
    update = inverse_diag * current / CHEB_CENTRE
    iterate = iterate + update
    for _ in range(degree - 1):
        rho_next = 1.0 / (2.0 * sigma_value - rho_prev)
        current = target - operate(iterate)
        update = rho_next * rho_prev * update + 2.0 * rho_next / CHEB_RADIUS * (
            inverse_diag * current
        )
        iterate = iterate + update
        rho_prev = rho_next
    return iterate


def inverse_diagonal(values):
    identity = jnp.eye(4, dtype=values.dtype)
    return 1.0 / jnp.sum(values[0] * identity[:, :, None], axis=1)


def split_parts(vector):
    high_part = vector.astype(jnp.bfloat16)
    rest_part = vector - lax.optimization_barrier(high_part).astype(jnp.float32)
    middle_part = rest_part.astype(jnp.bfloat16)
    low_part = (rest_part - lax.optimization_barrier(middle_part).astype(jnp.float32)).astype(
        jnp.bfloat16
    )
    return jnp.concatenate([high_part, middle_part, low_part], axis=0)


def join_parts(product, row_count):
    return product[:row_count] + product[row_count : 2 * row_count] + product[2 * row_count :]


def pick_columns(vector, index_flat):
    parts = split_parts(vector)
    width = parts.shape[1]
    total = index_flat.shape[0]
    block_size = math.gcd(total, 2048)
    places = jnp.arange(width, dtype=jnp.int32)[:, None]

    def one_block(index_block):
        select = (places == index_block[None, :]).astype(jnp.bfloat16)
        return jnp.dot(parts, select, preferred_element_type=jnp.float32)

    picked = lax.map(one_block, index_flat.reshape(total // block_size, block_size))
    picked = jnp.moveaxis(picked, 0, 1).reshape(parts.shape[0], total)
    return join_parts(picked, vector.shape[0])


def extend(vector, send_rows):
    halo_width = send_rows.shape[1]
    outgoing = pick_columns(vector, send_rows.reshape(-1)).reshape(4, 4, halo_width)
    stream_pair = jnp.concatenate([outgoing[:, 0], outgoing[:, 1]], axis=1)
    span_pair = jnp.concatenate([outgoing[:, 2], outgoing[:, 3]], axis=1)
    stream_ext = padded(stream_pair, (("stream", 1),), halo_width, True)
    span_ext = padded(span_pair, (("span", 1),), halo_width, False)
    return jnp.concatenate(
        [
            vector,
            stream_ext[:, :halo_width],
            stream_ext[:, 3 * halo_width :],
            span_ext[:, :halo_width],
            span_ext[:, 3 * halo_width :],
        ],
        axis=1,
    )


def block_product(values, gathered):
    return jnp.einsum("kijn,jkn->in", values, gathered, precision=lax.Precision.HIGHEST)


def apply_level(vector, values, columns, send_rows):
    extended_vec = extend(vector, send_rows)
    picked = pick_columns(extended_vec, columns.reshape(-1)).reshape(
        4, columns.shape[0], columns.shape[1]
    )
    return block_product(values, picked)


def membership(order_rows):
    row_count = order_rows.shape[0]
    grouped = order_rows.reshape(row_count // 4, 4)
    places = jnp.arange(row_count, dtype=jnp.int32)[:, None, None]
    return jnp.any(places == grouped[None, :, :], axis=2).astype(jnp.bfloat16)


def restrict(fine_vec, weights, member):
    product = jnp.einsum("ijn,in->jn", weights, fine_vec, precision=lax.Precision.HIGHEST)
    parts = split_parts(product)
    return join_parts(jnp.dot(parts, member, preferred_element_type=jnp.float32), 4)


def prolong(coarse, weights, member):
    parts = split_parts(coarse)
    spread = join_parts(
        lax.dot_general(
            parts, member, (((1,), (1,)), ((), ())), preferred_element_type=jnp.float32
        ),
        4,
    )
    return jnp.einsum("ijn,jn->in", weights, spread, precision=lax.Precision.HIGHEST)


def per_device(
    right_side,
    fine_values,
    fine_columns,
    fine_sends,
    fine_order,
    fine_weights,
    middle_values,
    middle_columns,
    middle_sends,
    middle_order,
    middle_weights,
    coarsest_values,
    coarsest_columns,
):

    def fine_apply(vector):
        return apply_level(vector, fine_values, fine_columns, fine_sends)

    def middle_apply(vector):
        return apply_level(vector, middle_values, middle_columns, middle_sends)

    fine_inv = inverse_diagonal(fine_values)
    middle_inv = inverse_diagonal(middle_values)
    fine_member = membership(fine_order[0])
    middle_member = membership(middle_order[0])
    first_iter = chebyshev(fine_apply, fine_inv, right_side, None, KSM)
    fine_resid = right_side - fine_apply(first_iter)
    middle_rhs = restrict(fine_resid, fine_weights, fine_member)
    middle_iter = chebyshev(middle_apply, middle_inv, middle_rhs, None, KSM)
    middle_resid = middle_rhs - middle_apply(middle_iter)
    coarse_rhs = restrict(middle_resid, middle_weights, middle_member)
    own_rows = coarse_rhs.shape[1]
    group_rhs, group_values = (
        lax.all_gather(coarse_rhs, "span", axis=1, tiled=True),
        lax.all_gather(coarsest_values, "span", axis=3, tiled=True),
    )
    group_columns = lax.all_gather(coarsest_columns, "span", axis=1, tiled=True)

    def group_apply(vector):
        return block_product(group_values, vector[:, group_columns])

    group_iter = chebyshev(group_apply, inverse_diagonal(group_values), group_rhs, None, KC)
    coarse_iter = lax.dynamic_slice_in_dim(
        group_iter, lax.axis_index("span") * own_rows, own_rows, 1
    )
    middle_start = middle_iter + prolong(coarse_iter, middle_weights, middle_member)
    middle_final = chebyshev(middle_apply, middle_inv, middle_rhs, middle_start, KSM)
    fine_start = first_iter + prolong(middle_final, fine_weights, fine_member)
    solution = chebyshev(fine_apply, fine_inv, right_side, fine_start, KSM)
    residual = right_side - fine_apply(solution)
    return (solution, residual)


def solution(mesh):
    in_specs = (
        P(None, ("stream", "span")),
        P(None, None, None, ("stream", "span")),
        P(None, ("stream", "span")),
        P(None, ("stream", "span")),
        P(("stream", "span"), None),
        P(None, None, ("stream", "span")),
        P(None, None, None, ("stream", "span")),
        P(None, ("stream", "span")),
        P(None, ("stream", "span")),
        P(("stream", "span"), None),
        P(None, None, ("stream", "span")),
        P(None, None, None, ("stream", "span")),
        P(None, ("stream", "span")),
    )
    out_specs = (P(None, ("stream", "span")), P(None, ("stream", "span")))
    return jax.shard_map(
        per_device, mesh=mesh, in_specs=in_specs, out_specs=out_specs, check_vma=False
    )
```

profile of v0, /device:TPU:1, one launch (start us, length us, event | category | flops | bytes accessed | tf_op | source)
XLA Modules:
  0.0 694.1 jit_solution(7039340005807783666)
XLA Ops:
  10.9 48.5 %all-gather.2.cloned.1.call-done = f32[8,4,4,2048]{3,2,1,0:T(4,128)} async-done(((f32[8,4,4,128]{3,2,1,0:T(4,128)}), f32[8,4,4,2048]{3,2,1,0:T(4,128)}) %all-gather.2.cloned.1.call-update) | async-done | bytes 1048592 | tf_op jit(solution)/shard_map/all_gather | solution.py:180
  71.2 6.1 fusion.78
  77.6 30.0 %while.39 = (s32[]{:T(128)}, f32[8,12,2048]{2,1,0:T(8,128)S(1)}, s32[8,2048]{1,0:T(8,128)}, bf16[12,2304]{1,0:T(8,128)(2,1)S(1)}, s32[]{:T(128)}) while((s32[]{:T(128)}, f32[8,12,2048]{2,1,0:T(8,128)S(1)}, s32[8,2048]{1,0:T(8,128)}, bf16[12,2304]{1,0:T(8,128)(2,1)S(1)}, s32[]{:T(128)}) %tuple.301), condition=%wide.region_2.0_spmd.clone, body=%wide.region_1.0_spmd.clone.sunk | while | flops 117964800 | bytes 229445 | solution.py:85
  112.6 5.7 collective-permute-start.6
  125.0 23.3 %while.40 = (s32[]{:T(128)}, f32[8,12,2048]{2,1,0:T(8,128)S(1)}, s32[8,2048]{1,0:T(8,128)S(1)}, bf16[12,2304]{1,0:T(8,128)(2,1)S(1)}, s32[]{:T(128)}) while((s32[]{:T(128)}, f32[8,12,2048]{2,1,0:T(8,128)S(1)}, s32[8,2048]{1,0:T(8,128)S(1)}, bf16[12,2304]{1,0:T(8,128)(2,1)S(1)}, s32[]{:T(128)}) %tuple.347), condition=%wide.region_4.5_spmd.clone, body=%wide.region_3.0_spmd.clone.sunk | while | flops 117964800 | bytes 229445 | solution.py:85
  157.7 26.1 %all_gather.11 = s32[8,2048]{1,0:T(8,128)} all-gather(s32[8,128]{1,0:T(8,128)S(1)} %copy-done.30), channel_id=1, replica_groups=mesh['stream'=8,'span'=16] {'span'}, dimensions={1}, use_global_device_ids=true | all-gather | bytes 69632 | tf_op jit(solution)/shard_map/all_gather | solution.py:182
  185.4 30.5 %while.41 = (s32[]{:T(128)}, f32[8,12,2048]{2,1,0:T(8,128)S(1)}, s32[8,2048]{1,0:T(8,128)S(1)}, bf16[12,2304]{1,0:T(8,128)(2,1)}, s32[]{:T(128)}) while((s32[]{:T(128)}, f32[8,12,2048]{2,1,0:T(8,128)S(1)}, s32[8,2048]{1,0:T(8,128)S(1)}, bf16[12,2304]{1,0:T(8,128)(2,1)}, s32[]{:T(128)}) %tuple.348), condition=%wide.region_7.8_spmd.clone, body=%wide.region_6.7_spmd.clone.sunk | while | flops 117964800 | bytes 211013 | solution.py:85
  222.0 5.4 collective-permute-start.14
  268.6 19.3 %all_gather.10 = f32[4,2048]{1,0:T(4,128)S(1)} all-gather(f32[4,128]{1,0:T(4,128)S(1)} %slice_add_fusion.58), channel_id=1, replica_groups=mesh['stream'=8,'span'=16] {'span'}, dimensions={1}, use_global_device_ids=true | all-gather | bytes 34816 | tf_op jit(solution)/shard_map/all_gather | solution.py:179
  289.0 54.8 %gather_fusion = f32[16384,4]{1,0:T(8,128)} fusion(f32[4,2048]{0,1:T(8,128)S(1)} %copy.181, s32[16384]{0:T(1024)S(1)} %broadcast_clamp_fusion), kind=kCustom, calls=%fused_computation | custom fusion | bytes 589824 | tf_op jit(solution)/shard_map/gather | solution.py:185
  343.8 5.3 copy.404
  351.8 60.0 %gather_fusion.1 = f32[16384,4]{1,0:T(8,128)} fusion(f32[4,2048]{0,1:T(8,128)S(1)} %copy.182, s32[16384]{0:T(1024)} %copy-done.5), kind=kCustom, calls=%fused_computation.1 | custom fusion | bytes 589824 | tf_op jit(solution)/shard_map/gather | solution.py:185
  411.8 5.2 copy.405
  419.2 60.0 %gather_fusion.2 = f32[16384,4]{1,0:T(8,128)} fusion(f32[4,2048]{0,1:T(8,128)S(1)} %copy.183, s32[16384]{0:T(1024)} %copy-done.5), kind=kCustom, calls=%fused_computation.2 | custom fusion | bytes 589824 | tf_op jit(solution)/shard_map/gather | solution.py:185
  479.3 5.3 copy.406
  510.2 4.4 collective-permute-done.31
  542.7 5.0 collective-permute-done.39
  548.0 23.3 %while.48 = (s32[]{:T(128)}, f32[8,12,2048]{2,1,0:T(8,128)S(1)}, s32[8,2048]{1,0:T(8,128)S(1)}, bf16[12,2304]{1,0:T(8,128)(2,1)S(1)}, s32[]{:T(128)}) while((s32[]{:T(128)}, f32[8,12,2048]{2,1,0:T(8,128)S(1)}, s32[8,2048]{1,0:T(8,128)S(1)}, bf16[12,2304]{1,0:T(8,128)(2,1)S(1)}, s32[]{:T(128)}) %tuple.349), condition=%wide.region_24.25_spmd.clone, body=%wide.region_23.24_spmd.clone.sunk | while | flops 117964800 | bytes 229445 | solution.py:85
  580.5 5.3 collective-permute-done.43
  586.1 23.3 %while.49 = (s32[]{:T(128)}, f32[8,12,2048]{2,1,0:T(8,128)S(1)}, s32[8,2048]{1,0:T(8,128)S(1)}, bf16[12,2304]{1,0:T(8,128)(2,1)S(1)}, s32[]{:T(128)}) while((s32[]{:T(128)}, f32[8,12,2048]{2,1,0:T(8,128)S(1)}, s32[8,2048]{1,0:T(8,128)S(1)}, bf16[12,2304]{1,0:T(8,128)(2,1)S(1)}, s32[]{:T(128)}) %tuple.350), condition=%wide.region_26.27_spmd.clone, body=%wide.region_25.26_spmd.clone.sunk | while | flops 117964800 | bytes 229445 | solution.py:85
  618.9 5.1 collective-permute-done.47
  624.3 23.3 %while.50 = (s32[]{:T(128)}, f32[8,12,2048]{2,1,0:T(8,128)S(1)}, s32[8,2048]{1,0:T(8,128)S(1)}, bf16[12,2304]{1,0:T(8,128)(2,1)S(1)}, s32[]{:T(128)}) while((s32[]{:T(128)}, f32[8,12,2048]{2,1,0:T(8,128)S(1)}, s32[8,2048]{1,0:T(8,128)S(1)}, bf16[12,2304]{1,0:T(8,128)(2,1)S(1)}, s32[]{:T(128)}) %tuple.351), condition=%wide.region_28.29_spmd.clone, body=%wide.region_27.28_spmd.clone.sunk | while | flops 117964800 | bytes 229445 | solution.py:85
  656.8 5.3 collective-permute-done.51
  662.5 23.3 %while.51 = (s32[]{:T(128)}, f32[8,12,2048]{2,1,0:T(8,128)S(1)}, s32[8,2048]{1,0:T(8,128)S(1)}, bf16[12,2304]{1,0:T(8,128)(2,1)S(1)}, s32[]{:T(128)}) while((s32[]{:T(128)}, f32[8,12,2048]{2,1,0:T(8,128)S(1)}, s32[8,2048]{1,0:T(8,128)S(1)}, bf16[12,2304]{1,0:T(8,128)(2,1)S(1)}, s32[]{:T(128)}) %tuple.352), condition=%wide.region_30.31_spmd.clone, body=%wide.region_29.30_spmd.clone.sunk | while | flops 117964800 | bytes 229445 | solution.py:85
  (582 shorter events, 362.8 us)
Async XLA Ops:
  7.2 52.2 %all-gather.2.cloned.1.call-start = ((), (), s32[]{:S(2)}) async-start(), calls=%async_computation | async-start | bytes 1114112 | tf_op jit(solution)/shard_map/all_gather | solution.py:180
  62.6 14.6 %collective-permute-start = (f32[4,64]{1,0:T(4,128)S(1)}, f32[4,64]{1,0:T(4,128)S(1)}, u32[]{:S(2)}, u32[]{:S(2)}) collective-permute-start(f32[4,64]{1,0:T(4,128)S(1)} %bitcast.712), channel_id=1, source_target_pairs={{0,16},{16,32},{32,48},{48,64},{64,80},{80,96},{96,112},{112,0},{1... | collective-permute-start | bytes 3080 | tf_op jit(solution)/shard_map/ppermute | solution.py:24
  63.1 14.2 %collective-permute-start.1 = (f32[4,64]{1,0:T(4,128)S(1)}, f32[4,64]{1,0:T(4,128)S(1)}, u32[]{:S(2)}, u32[]{:S(2)}) collective-permute-start(f32[4,64]{1,0:T(4,128)S(1)} %bitcast.701), channel_id=1, source_target_pairs={{16,0},{32,16},{48,32},{64,48},{80,64},{96,80},{112,96},{0,112},{1... | collective-permute-start | bytes 3080 | tf_op jit(solution)/shard_map/ppermute | solution.py:26
  66.3 11.0 %collective-permute-start.2 = (f32[4,64]{1,0:T(4,128)S(1)}, f32[4,64]{1,0:T(4,128)S(1)}, u32[]{:S(2)}, u32[]{:S(2)}) collective-permute-start(f32[4,64]{1,0:T(4,128)S(1)} %bitcast.689), channel_id=1, source_target_pairs={{0,1},{1,2},{2,3},{3,4},{4,5},{5,6},{6,7},{7,8},{8,9},{9,10},{10,1... | collective-permute-start | bytes 3080 | tf_op jit(solution)/shard_map/ppermute | solution.py:24
  108.8 11.6 %collective-permute-start.4 = (f32[4,64]{1,0:T(4,128)S(1)}, f32[4,64]{1,0:T(4,128)S(1)}, u32[]{:S(2)}, u32[]{:S(2)}) collective-permute-start(f32[4,64]{1,0:T(4,128)S(1)} %bitcast.713), channel_id=1, source_target_pairs={{0,16},{16,32},{32,48},{48,64},{64,80},{80,96},{96,112},{112,0},{1... | collective-permute-start | bytes 3080 | tf_op jit(solution)/shard_map/ppermute | solution.py:24
  108.8 11.5 %collective-permute-start.5 = (f32[4,64]{1,0:T(4,128)S(1)}, f32[4,64]{1,0:T(4,128)S(1)}, u32[]{:S(2)}, u32[]{:S(2)}) collective-permute-start(f32[4,64]{1,0:T(4,128)S(1)} %bitcast.702), channel_id=1, source_target_pairs={{16,0},{32,16},{48,32},{64,48},{80,64},{96,80},{112,96},{0,112},{1... | collective-permute-start | bytes 3080 | tf_op jit(solution)/shard_map/ppermute | solution.py:26
  149.5 34.9 %collective-permute-start.10 = (f32[4,64]{1,0:T(4,128)S(1)}, f32[4,64]{1,0:T(4,128)S(1)}, u32[]{:S(2)}, u32[]{:S(2)}) collective-permute-start(f32[4,64]{1,0:T(4,128)S(1)} %bitcast.714), channel_id=1, source_target_pairs={{0,1},{1,2},{2,3},{3,4},{4,5},{5,6},{6,7},{7,8},{8,9},{9,10},{10,1... | collective-permute-start | bytes 3080 | tf_op jit(solution)/shard_map/ppermute | solution.py:24
  152.1 32.3 %collective-permute-start.11 = (f32[4,64]{1,0:T(4,128)S(1)}, f32[4,64]{1,0:T(4,128)S(1)}, u32[]{:S(2)}, u32[]{:S(2)}) collective-permute-start(f32[4,64]{1,0:T(4,128)S(1)} %bitcast.703), channel_id=1, source_target_pairs={{1,0},{2,1},{3,2},{4,3},{5,4},{6,5},{7,6},{8,7},{9,8},{10,9},{11,1... | collective-permute-start | bytes 3080 | tf_op jit(solution)/shard_map/ppermute | solution.py:26
  154.0 30.4 %collective-permute-start.8 = (f32[4,64]{1,0:T(4,128)S(1)}, f32[4,64]{1,0:T(4,128)S(1)}, u32[]{:S(2)}, u32[]{:S(2)}) collective-permute-start(f32[4,64]{1,0:T(4,128)S(1)} %bitcast.691), channel_id=1, source_target_pairs={{0,16},{16,32},{32,48},{48,64},{64,80},{80,96},{96,112},{112,0},{1... | collective-permute-start | bytes 3080 | tf_op jit(solution)/shard_map/ppermute | solution.py:24
  154.1 30.3 %collective-permute-start.9 = (f32[4,64]{1,0:T(4,128)S(1)}, f32[4,64]{1,0:T(4,128)S(1)}, u32[]{:S(2)}, u32[]{:S(2)}) collective-permute-start(f32[4,64]{1,0:T(4,128)S(1)} %bitcast.680), channel_id=1, source_target_pairs={{16,0},{32,16},{48,32},{64,48},{80,64},{96,80},{112,96},{0,112},{1... | collective-permute-start | bytes 3080 | tf_op jit(solution)/shard_map/ppermute | solution.py:26
  218.3 13.0 %collective-permute-start.12 = (f32[4,64]{1,0:T(4,128)S(1)}, f32[4,64]{1,0:T(4,128)S(1)}, u32[]{:S(2)}, u32[]{:S(2)}) collective-permute-start(f32[4,64]{1,0:T(4,128)S(1)} %bitcast.704), channel_id=1, source_target_pairs={{0,16},{16,32},{32,48},{48,64},{64,80},{80,96},{96,112},{112,0},{1... | collective-permute-start | bytes 3080 | tf_op jit(solution)/shard_map/ppermute | solution.py:24
  218.4 12.9 %collective-permute-start.13 = (f32[4,64]{1,0:T(4,128)S(1)}, f32[4,64]{1,0:T(4,128)S(1)}, u32[]{:S(2)}, u32[]{:S(2)}) collective-permute-start(f32[4,64]{1,0:T(4,128)S(1)} %bitcast.692), channel_id=1, source_target_pairs={{16,0},{32,16},{48,32},{64,48},{80,64},{96,80},{112,96},{0,112},{1... | collective-permute-start | bytes 3080 | tf_op jit(solution)/shard_map/ppermute | solution.py:26
  222.0 9.3 %collective-permute-start.14 = (f32[4,64]{1,0:T(4,128)S(1)}, f32[4,64]{1,0:T(4,128)S(1)}, u32[]{:S(2)}, u32[]{:S(2)}) collective-permute-start(f32[4,64]{1,0:T(4,128)S(1)} %bitcast.681), channel_id=1, source_target_pairs={{0,1},{1,2},{2,3},{3,4},{4,5},{5,6},{6,7},{7,8},{8,9},{9,10},{10,1... | collective-permute-start | bytes 3080 | tf_op jit(solution)/shard_map/ppermute | solution.py:24
  236.8 9.7 %collective-permute-start.16 = (f32[4,64]{1,0:T(4,128)S(1)}, f32[4,64]{1,0:T(4,128)S(1)}, u32[]{:S(2)}, u32[]{:S(2)}) collective-permute-start(f32[4,64]{1,0:T(4,128)S(1)} %bitcast.693), channel_id=1, source_target_pairs={{0,16},{16,32},{32,48},{48,64},{64,80},{80,96},{96,112},{112,0},{1... | collective-permute-start | bytes 3080 | tf_op jit(solution)/shard_map/ppermute | solution.py:24
  236.9 9.7 %collective-permute-start.17 = (f32[4,64]{1,0:T(4,128)S(1)}, f32[4,64]{1,0:T(4,128)S(1)}, u32[]{:S(2)}, u32[]{:S(2)}) collective-permute-start(f32[4,64]{1,0:T(4,128)S(1)} %bitcast.682), channel_id=1, source_target_pairs={{16,0},{32,16},{48,32},{64,48},{80,64},{96,80},{112,96},{0,112},{1... | collective-permute-start | bytes 3080 | tf_op jit(solution)/shard_map/ppermute | solution.py:26
  253.1 8.2 %collective-permute-start.20 = (f32[4,64]{1,0:T(4,128)S(1)}, f32[4,64]{1,0:T(4,128)S(1)}, u32[]{:S(2)}, u32[]{:S(2)}) collective-permute-start(f32[4,64]{1,0:T(4,128)S(1)} %bitcast.674), channel_id=1, source_target_pairs={{0,16},{16,32},{32,48},{48,64},{64,80},{80,96},{96,112},{112,0},{1... | collective-permute-start | bytes 3080 | tf_op jit(solution)/shard_map/ppermute | solution.py:24
  253.2 8.2 %collective-permute-start.21 = (f32[4,64]{1,0:T(4,128)S(1)}, f32[4,64]{1,0:T(4,128)S(1)}, u32[]{:S(2)}, u32[]{:S(2)}) collective-permute-start(f32[4,64]{1,0:T(4,128)S(1)} %bitcast.673), channel_id=1, source_target_pairs={{16,0},{32,16},{48,32},{64,48},{80,64},{96,80},{112,96},{0,112},{1... | collective-permute-start | bytes 3080 | tf_op jit(solution)/shard_map/ppermute | solution.py:26
  486.2 8.6 %collective-permute-start.24 = (f32[4,64]{1,0:T(4,128)S(1)}, f32[4,64]{1,0:T(4,128)S(1)}, u32[]{:S(2)}, u32[]{:S(2)}) collective-permute-start(f32[4,64]{1,0:T(4,128)S(1)} %bitcast.716), channel_id=1, source_target_pairs={{0,16},{16,32},{32,48},{48,64},{64,80},{80,96},{96,112},{112,0},{1... | collective-permute-start | bytes 3080 | tf_op jit(solution)/shard_map/ppermute | solution.py:24
  486.3 8.5 %collective-permute-start.25 = (f32[4,64]{1,0:T(4,128)S(1)}, f32[4,64]{1,0:T(4,128)S(1)}, u32[]{:S(2)}, u32[]{:S(2)}) collective-permute-start(f32[4,64]{1,0:T(4,128)S(1)} %bitcast.706), channel_id=1, source_target_pairs={{16,0},{32,16},{48,32},{64,48},{80,64},{96,80},{112,96},{0,112},{1... | collective-permute-start | bytes 3080 | tf_op jit(solution)/shard_map/ppermute | solution.py:26
  502.1 8.1 %collective-permute-start.28 = (f32[4,64]{1,0:T(4,128)S(1)}, f32[4,64]{1,0:T(4,128)S(1)}, u32[]{:S(2)}, u32[]{:S(2)}) collective-permute-start(f32[4,64]{1,0:T(4,128)S(1)} %bitcast.717), channel_id=1, source_target_pairs={{0,16},{16,32},{32,48},{48,64},{64,80},{80,96},{96,112},{112,0},{1... | collective-permute-start | bytes 3080 | tf_op jit(solution)/shard_map/ppermute | solution.py:24
  534.4 8.3 %collective-permute-start.36 = (f32[4,64]{1,0:T(4,128)S(1)}, f32[4,64]{1,0:T(4,128)S(1)}, u32[]{:S(2)}, u32[]{:S(2)}) collective-permute-start(f32[4,64]{1,0:T(4,128)S(1)} %bitcast.719), channel_id=1, source_target_pairs={{0,16},{16,32},{32,48},{48,64},{64,80},{80,96},{96,112},{112,0},{1... | collective-permute-start | bytes 3080 | tf_op jit(solution)/shard_map/ppermute | solution.py:24
  534.5 8.2 %collective-permute-start.37 = (f32[4,64]{1,0:T(4,128)S(1)}, f32[4,64]{1,0:T(4,128)S(1)}, u32[]{:S(2)}, u32[]{:S(2)}) collective-permute-start(f32[4,64]{1,0:T(4,128)S(1)} %bitcast.709), channel_id=1, source_target_pairs={{16,0},{32,16},{48,32},{64,48},{80,64},{96,80},{112,96},{0,112},{1... | collective-permute-start | bytes 3080 | tf_op jit(solution)/shard_map/ppermute | solution.py:26
  610.5 8.3 %collective-permute-start.44 = (f32[4,64]{1,0:T(4,128)S(1)}, f32[4,64]{1,0:T(4,128)S(1)}, u32[]{:S(2)}, u32[]{:S(2)}) collective-permute-start(f32[4,64]{1,0:T(4,128)S(1)} %bitcast.721), channel_id=1, source_target_pairs={{0,16},{16,32},{32,48},{48,64},{64,80},{80,96},{96,112},{112,0},{1... | collective-permute-start | bytes 3080 | tf_op jit(solution)/shard_map/ppermute | solution.py:24
  610.6 8.3 %collective-permute-start.45 = (f32[4,64]{1,0:T(4,128)S(1)}, f32[4,64]{1,0:T(4,128)S(1)}, u32[]{:S(2)}, u32[]{:S(2)}) collective-permute-start(f32[4,64]{1,0:T(4,128)S(1)} %bitcast.711), channel_id=1, source_target_pairs={{16,0},{32,16},{48,32},{64,48},{80,64},{96,80},{112,96},{0,112},{1... | collective-permute-start | bytes 3080 | tf_op jit(solution)/shard_map/ppermute | solution.py:26
  (67 other events, 1012.0 us)
Sparse Core Ops, SparseCore 0:
  10.3 49.1 all-gather.1
where the time goes:
time: 707 us; the launch traced here: 694 us
  local copies, waits for them, and re-layouts  209 us (30%)
  matrix products  188 us (27%)
  starting transfers between devices  114 us (16%)
  waiting for transfers between devices  97.8 us (14%)
  blocking collectives  45.4 us (6%)
  other arithmetic  22.8 us (3%)
  between operations  16.7 us (2%)
    dot_general x81, matrix products, one_block(): return jnp.dot(parts, select, preferred_element_type=jnp.float32)  187 us
    gather x3, local copies, waits for them, and re-layouts, group_apply(): return block_product(group_values, vector[:, group_columns])  175 us
    ppermute x26, starting transfers between devices, padded(): lax.ppermute(head, axis, [((i + 1) % count, i) for i in range(ends)])  72.1 us
    ppermute x26, waiting for transfers between devices, padded(): lax.ppermute(head, axis, [((i + 1) % count, i) for i in range(ends)])  48.6 us
    all_gather x1, waiting for transfers between devices, per_device(): lax.all_gather(coarsest_values, 'span', axis=3, tiled=True)  48.5 us
    ppermute x26, starting transfers between devices, padded(): lax.ppermute(tail, axis, [(i, (i + 1) % count) for i in range(ends)])  41.5 us
    all_gather x1, blocking collectives, per_device(): group_columns = lax.all_gather(coarsest_columns, 'span', axis=1, tiled=True)  26.1 us
    all_gather x1, blocking collectives, per_device(): lax.all_gather(coarse_rhs, 'span', axis=1, tiled=True)  19.3 us
  transfers between devices with their start and end apart: 53, of which 12 were waited for; matrix products, arithmetic and copies ran while one was open for 2% of the time, Pallas kernels for 0%

commit v1 on v0

v1 whole, which is shorter than its diff:
```python
import functools

import jax
import jax.numpy as jnp
from jax import lax
from jax.experimental import pallas as pl
from jax.experimental.pallas import tpu as pltpu
from jax.sharding import PartitionSpec as P

KSM = 3
KC = 4
CHEB_CENTRE = 1.0
CHEB_RADIUS = 0.9
LANES = 128
HALF = 64
MESH = pl.DeviceIdType.MESH


def chebyshev_factors(degree):
    sigma_value = CHEB_CENTRE / CHEB_RADIUS
    rho_prev = 1.0 / sigma_value
    factors = []
    for _ in range(degree - 1):
        rho_next = 1.0 / (2.0 * sigma_value - rho_prev)
        factors.append((rho_next * rho_prev, 2.0 * rho_next / CHEB_RADIUS))
        rho_prev = rho_next
    return factors


def gather_lanes(table, places):
    return jnp.take_along_axis(table, places, axis=1, mode="promise_in_bounds")


def row_of(ref, row):
    return jnp.broadcast_to(ref[pl.ds(row, 1), :], (8, LANES))


def lookup(tables, low, high, base=0, start=None):
    picked = start
    for h, table in enumerate(tables):
        taken = gather_lanes(table, low)
        picked = taken if picked is None else jnp.where(high == h + base, taken, picked)
    return picked


def cycle_kernel(
    tiles1, tiles2, streams, spans,
    right_hbm, values1_hbm, columns1_hbm, sends1_hbm, order1_hbm, weights1_hbm,
    values2_hbm, columns2_hbm, sends2_hbm, order2_hbm, weights2_hbm,
    values3_hbm, columns3_hbm,
    solution_ref, residual_ref,
    right_in, values1_in, columns1_in, sends1_in, order1_in, weights1_in,
    values2_in, columns2_in, sends2_in, order2_in, weights2_in,
    values3_in, columns3_in,
    right1, values1, columns1, picks1, restrict1, prolong1, weights1, inv1,
    values2, columns2, picks2, restrict2, prolong2, weights2, inv2,
    order_rows, table1, table2, first1, first2, right2, part1, part2, product1, product2,
    outgoing, incoming, halo, gathered, group_own, group_all, table3, inv3,
    in_sem, send_sem, recv_sem, group_send_sem, group_recv_sem,
):
    a = lax.axis_index("stream")
    b = lax.axis_index("span")
    prev_a, next_a = lax.rem(a + streams - 1, streams), lax.rem(a + 1, streams)
    prev_b, next_b = lax.rem(b + spans - 1, spans), lax.rem(b + 1, spans)

    barrier = pltpu.get_barrier_semaphore()
    for who in (prev_a, next_a):
        pl.semaphore_signal(barrier, inc=1, device_id=(who, b), device_id_type=MESH)
    for step in range(1, spans):
        pl.semaphore_signal(
            barrier, inc=1, device_id=(a, lax.rem(b + step, spans)), device_id_type=MESH
        )

    loads = [
        pltpu.make_async_copy(src, dst, in_sem.at[n])
        for n, (src, dst) in enumerate(
            (
                (right_hbm, right_in), (values1_hbm, values1_in), (columns1_hbm, columns1_in),
                (sends1_hbm, sends1_in), (order1_hbm, order1_in), (weights1_hbm, weights1_in),
                (values2_hbm, values2_in), (columns2_hbm, columns2_in), (sends2_hbm, sends2_in),
                (order2_hbm, order2_in), (weights2_hbm, weights2_in),
                (values3_hbm, values3_in), (columns3_hbm, columns3_in),
            )
        )
    ]
    for load in loads:
        load.start()
    for load in loads:
        load.wait()

    lane = lax.broadcasted_iota(jnp.int32, (8, LANES), 1)
    row = lax.broadcasted_iota(jnp.int32, (8, LANES), 0)

    def dense_blocks(source, target, tiles):
        for k in range(8):
            for i in range(4):
                for t in range(tiles):
                    target[pl.ds((k * 16 + i * 4) * tiles + t, 4, stride=tiles), :] = source[
                        k, i, :, t * LANES : (t + 1) * LANES
                    ]

    def dense_weights(source, target, tiles):
        for i in range(4):
            for t in range(tiles):
                target[pl.ds(i * 4 * tiles + t, 4, stride=tiles), :] = source[
                    i, :, t * LANES : (t + 1) * LANES
                ]

    dense_blocks(values1_in, values1, tiles1)
    for t in range(tiles1):
        right1[pl.ds(t, 4, stride=tiles1), :] = right_in[:, t * LANES : (t + 1) * LANES]
        columns1[pl.ds(t, 8, stride=tiles1), :] = columns1_in[:, t * LANES : (t + 1) * LANES]
    for i in range(4):
        inv1[pl.ds(i * tiles1, tiles1), :] = 1.0 / values1[pl.ds(i * 5 * tiles1, tiles1), :]

    def pick_places(sends):
        stream_part = jnp.concatenate([sends[1:2, :], sends[0:1, :]], axis=1)
        span_part = jnp.concatenate([sends[3:4, :], sends[2:3, :]], axis=1)
        return jnp.where(
            row < 4,
            jnp.broadcast_to(stream_part, (8, LANES)),
            jnp.broadcast_to(span_part, (8, LANES)),
        )

    picks1[...] = pick_places(sends1_in)
    picks2[...] = pick_places(sends2_in)

    for i in range(4):
        for k in range(8):
            for t in range(tiles2):
                values2[pl.ds(i * 32 * tiles2 + k * tiles2 + t, 4, stride=8 * tiles2), :] = (
                    values2_in[k, i, :, t * LANES : (t + 1) * LANES]
                )
    for t in range(tiles2):
        columns2[pl.ds(t, 8, stride=tiles2), :] = columns2_in[:, t * LANES : (t + 1) * LANES]
    for i in range(4):
        inv2[pl.ds(i * tiles2, tiles2), :] = 1.0 / values2[pl.ds(i * 5 * 8 * tiles2, tiles2), :]
    dense_weights(weights1_in, weights1, tiles1)
    dense_weights(weights2_in, weights2, tiles2)

    quad = lane // 32
    for t in range(tiles1):
        order_rows[pl.ds(t, 1), :] = order1_in[:, t * LANES : (t + 1) * LANES]
    for pair in range(2):
        entry = row // 4 + 2 * pair
        low = (lane * 4 + entry) % LANES
        found = None
        for q in range(4):
            rows = order_rows[pl.ds(q, 4, stride=4), :]
            taken = gather_lanes(jnp.concatenate([rows, rows], axis=0), low)
            found = taken if found is None else jnp.where(quad == q, taken, found)
        restrict1[pl.ds(pair * 8, 8), :] = found

    def inverse_order(rows_ref, count, tiles):
        total = jnp.zeros((2 * tiles, LANES), jnp.float32)
        for t in range(count):
            own = rows_ref[pl.ds(t, 1), :]
            tile_ids = lax.broadcasted_iota(jnp.int32, (tiles, LANES), 0)
            member = (jnp.broadcast_to(own // LANES, (tiles, LANES)) == tile_ids)
            lanes = lax.broadcasted_iota(jnp.int32, (tiles, LANES), 1)
            small = jnp.where(member, (lanes // 4).astype(jnp.float32), 0.0)
            large = jnp.where(member, float(t), 0.0)
            left = jnp.concatenate([small, large], axis=0)
            low_ids = lax.broadcasted_iota(jnp.int32, (LANES, LANES), 0)
            right = jnp.where(
                jnp.broadcast_to(own % LANES, (LANES, LANES)) == low_ids, 1.0, 0.0
            )
            total = total + lax.dot_general(
                left.astype(jnp.bfloat16),
                right.astype(jnp.bfloat16),
                (((1,), (1,)), ((), ())),
                preferred_element_type=jnp.float32,
            )
        return (total[:tiles] + 32.0 * total[tiles:]).astype(jnp.int32)

    prolong1[...] = inverse_order(order_rows, tiles1, tiles1)

    for t in range(tiles2):
        order_rows[pl.ds(t, 1), :] = order2_in[:, t * LANES : (t + 1) * LANES]
    low = (lane * 4 + row % 4) % LANES
    found = None
    for q in range(4):
        taken = gather_lanes(row_of(order_rows, q), low)
        found = taken if found is None else jnp.where(quad == q, taken, found)
    restrict2[...] = found
    prolong2[...] = inverse_order(order_rows, tiles2, 8)

    pl.semaphore_wait(barrier, spans + 1)

    sends = []

    def copies_of(x):
        places = (
            (1, (prev_a, b)),
            (0, (next_a, b)),
            (3, (a, prev_b)),
            (2, (a, next_b)),
        )
        return [
            pltpu.make_async_remote_copy(
                src_ref=outgoing.at[x],
                dst_ref=incoming.at[x, slot],
                send_sem=send_sem.at[x, slot],
                recv_sem=recv_sem.at[x, slot],
                device_id=who,
                device_id_type=MESH,
            )
            for slot, who in places
        ]

    def exchange_start(x, table, picks, tiles):
        places = picks[...]
        tables = [table[pl.ds(h, 8, stride=tiles), :] for h in range(tiles)]
        outgoing[x] = lookup(tables, places % LANES, places // LANES)
        for copy in copies_of(x):
            copy.start()
            sends.append(copy)

    def exchange_end(x):
        for copy in copies_of(x):
            copy.wait_recv()
        first_half = lane < HALF
        block2 = jnp.where(b > 0, incoming[x, 2], 0.0)
        block3 = jnp.where(b < spans - 1, incoming[x, 3], 0.0)
        halo[...] = jnp.where(
            row < 4,
            jnp.where(first_half, incoming[x, 0], incoming[x, 1]),
            jnp.where(first_half, block2, block3),
        )

    def store_table(table, vector, tiles):
        table[pl.ds(0, 4 * tiles), :] = vector
        table[pl.ds(4 * tiles, 4 * tiles), :] = vector

    def operate1(x):
        exchange_start(x, table1, picks1, tiles1)

        def local(group, carry):
            where_to = columns1[pl.ds(pl.multiple_of(group * 8, 8), 8), :]
            low, high = where_to % LANES, where_to // LANES
            for j in range(4):
                gathered[j, pl.ds(pl.multiple_of(group * 8, 8), 8), :] = lookup(
                    [row_of(table1, j * tiles1 + h) for h in range(tiles1)], low, high
                )
            return carry

        lax.fori_loop(0, tiles1, local, 0)
        exchange_end(x)

        def remote(part, carry):
            sums = [None] * 4
            for k in range(8):
                start = k * tiles1 + part * 8
                here = pl.ds(pl.multiple_of(start, 8), 8)
                where_to = columns1[here, :]
                low, high = where_to % LANES, where_to // LANES
                for j in range(4):
                    found = lookup(
                        [row_of(halo, j), row_of(halo, 4 + j)],
                        low, high, tiles1, gathered[j, here, :],
                    )
                    for i in range(4):
                        at = (k * 16 + i * 4 + j) * tiles1 + part * 8
                        term = values1[pl.ds(pl.multiple_of(at, 8), 8), :] * found
                        sums[i] = term if sums[i] is None else sums[i] + term
            for i in range(4):
                part1[pl.ds(pl.multiple_of(i * tiles1 + part * 8, 8), 8), :] = sums[i]
            return carry

        lax.fori_loop(0, tiles1 // 8, remote, 0)
        return part1[...]

    def operate2(x):
        exchange_start(x, table2, picks2, tiles2)
        groups = 8 * tiles2 // 8

        def local(group, carry):
            where_to = columns2[pl.ds(pl.multiple_of(group * 8, 8), 8), :]
            low, high = where_to % LANES, where_to // LANES
            for j in range(4):
                gathered[j, pl.ds(pl.multiple_of(group * 8, 8), 8), :] = lookup(
                    [row_of(table2, j * tiles2 + h) for h in range(tiles2)], low, high
                )
            return carry

        lax.fori_loop(0, groups, local, 0)
        exchange_end(x)
        sums = [None] * 4
        for group in range(groups):
            here = pl.ds(group * 8, 8)
            where_to = columns2[here, :]
            low, high = where_to % LANES, where_to // LANES
            for j in range(4):
                found = lookup(
                    [row_of(halo, j), row_of(halo, 4 + j)],
                    low, high, tiles2, gathered[j, here, :],
                )
                for i in range(4):
                    term = values2[pl.ds((i * 4 + j) * 8 * tiles2 + group * 8, 8), :] * found
                    sums[i] = term if sums[i] is None else sums[i] + term
        for i in range(4):
            part2[pl.ds(i * tiles2, tiles2), :] = sums[i][:4] + sums[i][4:]
        return part2[...]

    def smooth(operate, table, tiles, right, inv, first, x):
        if first:
            update = inv[...] * right[...]
            store_table(table, update, tiles)
        else:
            update = inv[...] * (right[...] - operate(x))
            x += 1
            store_table(table, table[pl.ds(0, 4 * tiles), :] + update, tiles)
        for keep, gain in chebyshev_factors(KSM):
            current = right[...] - operate(x)
            x += 1
            update = keep * update + gain * (inv[...] * current)
            store_table(table, table[pl.ds(0, 4 * tiles), :] + update, tiles)
        return x

    x = smooth(operate1, table1, tiles1, right1, inv1, True, 0)
    first1[...] = table1[pl.ds(0, 4 * tiles1), :]
    resid = right1[...] - operate1(x)
    x += 1
    part1[...] = resid
    for j in range(4):
        total = None
        for i in range(4):
            term = (
                weights1[pl.ds((i * 4 + j) * tiles1, tiles1), :]
                * part1[pl.ds(i * tiles1, tiles1), :]
            )
            total = term if total is None else total + term
        product1[pl.ds(j * tiles1, tiles1), :] = total
    for j in range(4):
        tables = [row_of(product1, j * tiles1 + h) for h in range(tiles1)]
        total = None
        for pair in range(2):
            where_to = restrict1[pl.ds(pair * 8, 8), :]
            taken = lookup(tables, where_to % LANES, where_to // LANES)
            total = taken if total is None else total + taken
        right2[pl.ds(j * tiles2, tiles2), :] = total[:4] + total[4:]

    x = smooth(operate2, table2, tiles2, right2, inv2, True, x)
    first2[...] = table2[pl.ds(0, 4 * tiles2), :]
    resid = right2[...] - operate2(x)
    x += 1
    part2[...] = resid
    for j in range(4):
        total = None
        for i in range(4):
            term = (
                weights2[pl.ds((i * 4 + j) * tiles2, tiles2), :]
                * part2[pl.ds(i * tiles2, tiles2), :]
            )
            total = term if total is None else total + term
        product2[pl.ds(j * tiles2, tiles2), :] = total
    where_to = restrict2[...]
    for j in range(4):
        tables = [row_of(product2, j * tiles2 + h) for h in range(tiles2)]
        taken = lookup(tables, where_to % LANES, where_to // LANES)
        table3[pl.ds(j, 1), :] = jnp.sum(taken[:4], axis=0, keepdims=True)

    right3 = table3[...]
    for i in range(4):
        inv3[pl.ds(i, 1), :] = 1.0 / values3_in[0, i, i : i + 1, :]
    update = inv3[...] * right3
    vector = update
    columns3 = columns3_in[...]
    low3, high3 = columns3 % LANES, columns3 // LANES
    for turn, (keep, gain) in enumerate(chebyshev_factors(KC)):
        group_own[turn] = vector
        copies = []
        for step in range(1, spans):
            copies.append(
                pltpu.make_async_remote_copy(
                    src_ref=group_own.at[turn],
                    dst_ref=group_all.at[turn, step],
                    send_sem=group_send_sem.at[turn, step],
                    recv_sem=group_recv_sem.at[turn, step],
                    device_id=(a, lax.rem(b + step, spans)),
                    device_id_type=MESH,
                )
            )
        for copy in copies:
            copy.start()
            sends.append(copy)
        for copy in copies:
            copy.wait_recv()
        distance = lax.rem(b - high3 + spans, spans)
        picked = []
        for j in range(4):
            tables = [row_of(group_own.at[turn], j)] + [
                row_of(group_all.at[turn, step], j) for step in range(1, spans)
            ]
            picked.append(lookup(tables, low3, distance))
        for i in range(4):
            total = None
            for j in range(4):
                term = values3_in[:, i, j, :] * picked[j]
                total = term if total is None else total + term
            table3[pl.ds(i, 1), :] = jnp.sum(total, axis=0, keepdims=True)
        current = right3 - table3[...]
        update = keep * update + gain * (inv3[...] * current)
        vector = vector + update

    table3[...] = vector
    back = prolong2[...]
    spread = [gather_lanes(row_of(table3, j), back) for j in range(4)]
    for i in range(4):
        total = first2[pl.ds(i * tiles2, tiles2), :]
        for j in range(4):
            total = total + weights2[pl.ds((i * 4 + j) * tiles2, tiles2), :] * spread[j][:tiles2]
        table2[pl.ds(i * tiles2, tiles2), :] = total
        table2[pl.ds((4 + i) * tiles2, tiles2), :] = total
    x = smooth(operate2, table2, tiles2, right2, inv2, False, x)

    for part in range(tiles1 // 8):
        where_to = prolong1[pl.ds(part * 8, 8), :]
        low, high = where_to % LANES, where_to // LANES
        spread = [
            lookup([row_of(table2, j * tiles2 + h) for h in range(tiles2)], low, high)
            for j in range(4)
        ]
        for i in range(4):
            total = first1[pl.ds(i * tiles1 + part * 8, 8), :]
            for j in range(4):
                total = (
                    total
                    + weights1[pl.ds((i * 4 + j) * tiles1 + part * 8, 8), :] * spread[j]
                )
            table1[pl.ds(i * tiles1 + part * 8, 8), :] = total
            table1[pl.ds((4 + i) * tiles1 + part * 8, 8), :] = total
    x = smooth(operate1, table1, tiles1, right1, inv1, False, x)
    solution_ref[...] = table1[pl.ds(0, 4 * tiles1), :]
    residual_ref[...] = right1[...] - operate1(x)

    for copy in sends:
        copy.wait_send()


def per_device(streams, spans, *arrays):
    right_side = arrays[0]
    rows1, rows2, rows3 = right_side.shape[1], arrays[9].shape[1], arrays[12].shape[1]
    tiles1, tiles2 = rows1 // LANES, rows2 // LANES
    exchanges = 4 * KSM + 1
    f32, i32 = jnp.float32, jnp.int32
    vmem = pltpu.VMEM
    scratch = [vmem(v.shape, v.dtype) for v in arrays]
    scratch += [
        vmem((4 * tiles1, LANES), f32),
        vmem((128 * tiles1, LANES), f32),
        vmem((8 * tiles1, LANES), i32),
        vmem((8, LANES), i32),
        vmem((16, LANES), i32),
        vmem((tiles1, LANES), i32),
        vmem((16 * tiles1, LANES), f32),
        vmem((4 * tiles1, LANES), f32),
        vmem((128 * tiles2, LANES), f32),
        vmem((8 * tiles2, LANES), i32),
        vmem((8, LANES), i32),
        vmem((8, LANES), i32),
        vmem((8, LANES), i32),
        vmem((16 * tiles2, LANES), f32),
        vmem((4 * tiles2, LANES), f32),
        vmem((tiles1, LANES), i32),
        vmem((8 * tiles1, LANES), f32),
        vmem((8 * tiles2, LANES), f32),
        vmem((4 * tiles1, LANES), f32),
        vmem((4 * tiles2, LANES), f32),
        vmem((4 * tiles2, LANES), f32),
        vmem((4 * tiles1, LANES), f32),
        vmem((4 * tiles2, LANES), f32),
        vmem((4 * tiles1, LANES), f32),
        vmem((4 * tiles2, LANES), f32),
        vmem((exchanges, 8, LANES), f32),
        vmem((exchanges, 4, 8, LANES), f32),
        vmem((8, LANES), f32),
        vmem((4, 8 * tiles1, LANES), f32),
        vmem((KC - 1, 4, LANES), f32),
        vmem((KC - 1, spans, 4, LANES), f32),
        vmem((4, LANES), f32),
        vmem((4, LANES), f32),
        pltpu.SemaphoreType.DMA((len(arrays),)),
        pltpu.SemaphoreType.DMA((exchanges, 4)),
        pltpu.SemaphoreType.DMA((exchanges, 4)),
        pltpu.SemaphoreType.DMA((KC - 1, spans)),
        pltpu.SemaphoreType.DMA((KC - 1, spans)),
    ]
    out = jax.ShapeDtypeStruct((4 * tiles1, LANES), f32)
    results = pl.pallas_call(
        functools.partial(cycle_kernel, tiles1, tiles2, streams, spans),
        out_shape=(out, out),
        in_specs=[pl.BlockSpec(memory_space=pl.ANY)] * len(arrays),
        out_specs=[pl.BlockSpec(memory_space=pltpu.VMEM)] * 2,
        scratch_shapes=scratch,
        compiler_params=pltpu.CompilerParams(
            collective_id=0, has_side_effects=True, vmem_limit_bytes=48 * 1024 * 1024
        ),
        name="cycle",
    )(*arrays)
    return tuple(r.reshape(4, rows1) for r in results)


def solution(mesh):
    both = ("stream", "span")
    in_specs = (
        P(None, both),
        P(None, None, None, both),
        P(None, both),
        P(None, both),
        P(both, None),
        P(None, None, both),
        P(None, None, None, both),
        P(None, both),
        P(None, both),
        P(both, None),
        P(None, None, both),
        P(None, None, None, both),
        P(None, both),
    )
    out_specs = (P(None, both), P(None, both))
    return jax.shard_map(
        functools.partial(per_device, mesh.shape["stream"], mesh.shape["span"]),
        mesh=mesh,
        in_specs=in_specs,
        out_specs=out_specs,
        check_vma=False,
    )
```

time: 707 us -> 92.5 us (0.13); the launches traced: 694 us -> 90.9 us
  local copies, waits for them, and re-layouts: 209 us -> 11.7 us
  matrix products: 188 us -> 0 us
  starting transfers between devices: 114 us -> 0 us
  waiting for transfers between devices: 97.8 us -> 0 us
  Pallas kernels: 0 us -> 78.5 us
  blocking collectives: 45.4 us -> 0 us
  other arithmetic: 22.8 us -> 0 us
  between operations: 16.7 us -> 0.66 us
    dot_general x85 -> x0, matrix products: 188 us -> none  [the longest x81 187 us: one_block(): return jnp.dot(parts, select, preferred_element_type=jnp.float32)]
    gather x3 -> x0, local copies, waits for them, and re-layouts: 175 us -> none  [group_apply(): return block_product(group_values, vector[:, group_columns])]
    ppermute x52 -> x0, starting transfers between devices: 114 us -> none  [the longest x26 72.1 us: padded(): lax.ppermute(head, axis, [((i + 1) % count, i) for i in range(ends)])]
    pallas_call x0 -> x1, Pallas kernels: none -> 78.5 us  [per_device(): pl.pallas_call(functools.partial(cycle_kernel, tiles1, tiles2, streams, s...]
    ppermute x52 -> x0, waiting for transfers between devices: 48.7 us -> none  [the longest x26 48.6 us: padded(): lax.ppermute(head, axis, [((i + 1) % count, i) for i in range(ends)])]
    all_gather x1 -> x0, waiting for transfers between devices: 48.5 us -> none  [per_device(): lax.all_gather(coarsest_values, 'span', axis=3, tiled=True)]
    all_gather x2 -> x0, blocking collectives: 45.4 us -> none  [the longest x1 26.1 us: per_device(): group_columns = lax.all_gather(coarsest_columns, 'span', axis=1, tiled=True)]
    dynamic_slice x68 -> x0, local copies, waits for them, and re-layouts: 7.53 us -> none  [pick_columns(): lax.map(one_block, index_flat.reshape(total // block_size, block_size))]
  transfers between devices with their start and end apart: 53 -> 0, of which waited for: 12 -> 0; matrix products, arithmetic and copies ran while one was open for 2% -> 0% of each run, Pallas kernels for 0% -> 0%
where the time goes in v1:
time: 92.5 us; the launch traced here: 90.9 us
  Pallas kernels  78.5 us (85%)
  local copies, waits for them, and re-layouts  11.7 us (13%)
    pallas_call x1, Pallas kernels, per_device(): pl.pallas_call(functools.partial(cycle_kernel, tiles1, tiles2, streams, s...  78.5 us
    unnamed x26, local copies, waits for them, and re-layouts  10.4 us

profile of v1, /device:TPU:1, one launch (start us, length us, event | category | flops | bytes accessed | tf_op | source)
XLA Modules:
  0.0 90.9 jit_solution(324467798260606991)
XLA Ops:
  0.6 0.0 copy-start
  0.6 1.2 %copy-done = f32[8,4,4,2048]{3,2,1,0:T(4,128)S(1)} copy-done((f32[8,4,4,2048]{3,2,1,0:T(4,128)S(1)}, f32[8,4,4,2048]{3,2,1,0:T(4,128)}, u32[]{:S(2)}) %copy-start) | copy-done | bytes 1048600
  1.9 0.0 copy-start.1
  1.9 0.9 %copy-done.1 = f32[8,4,4,512]{3,2,1,0:T(4,128)S(1)} copy-done((f32[8,4,4,512]{3,2,1,0:T(4,128)S(1)}, f32[8,4,4,512]{3,2,1,0:T(4,128)}, u32[]{:S(2)}) %copy-start.1) | copy-done | bytes 262168
  2.8 0.0 copy-start.2
  2.8 0.9 copy-done.2
  3.7 0.0 copy-start.3
  3.7 0.8 copy-done.3
  4.6 0.0 copy-start.4
  4.6 0.8 copy-done.4
  5.4 0.0 copy-start.5
  5.4 0.8 copy-done.5
  6.2 0.8 copy-done.6
  6.9 0.0 copy-start.7
  6.9 0.7 copy-done.7
  7.6 0.0 copy-start.8
  7.6 0.7 copy-done.8
  8.3 0.7 copy-done.9
  9.0 0.7 copy-done.10
  9.7 0.7 copy-done.11
  10.4 0.7 copy-done.12
  11.1 78.5 %cycle.1 = (f32[64,128]{1,0:T(8,128)S(1)}, f32[64,128]{1,0:T(8,128)S(1)}) custom-call(f32[4,2048]{1,0:T(4,128)S(1)} %copy-done.5, f32[8,4,4,2048]{3,2,1,0:T(4,128)S(1)} %copy-done, s32[8,2048]{1,0:T(8,128)S(1)} %copy-done.3, s32[4,64]{1,0:T(4,128)S(1)} %copy-done.10, s32[1,2048]{1,0:T(1,128)S(1)} %copy-done.8, f32[4,4,2048]{2,1,0:T(4,128)S(1)} %copy-done.2, ...), custom_call_target="tpu_custom_call" | custom-call | tf_op jit(solution)/shard_map/cycle/pallas_call | solution.py:490
  89.6 0.6 reshape.10
  90.2 0.6 reshape.11
  (5 shorter events, 0.0 us)
Async XLA Ops:
  0.6 1.2 %copy-start = (f32[8,4,4,2048]{3,2,1,0:T(4,128)S(1)}, f32[8,4,4,2048]{3,2,1,0:T(4,128)}, u32[]{:S(2)}) copy-start(f32[8,4,4,2048]{3,2,1,0:T(4,128)} %values1_hbm.1) | copy-start | bytes 3145732
  1.9 0.9 %copy-start.1 = (f32[8,4,4,512]{3,2,1,0:T(4,128)S(1)}, f32[8,4,4,512]{3,2,1,0:T(4,128)}, u32[]{:S(2)}) copy-start(f32[8,4,4,512]{3,2,1,0:T(4,128)} %values2_hbm.1) | copy-start | bytes 786436
  2.8 0.9 copy-start.2
  3.7 0.8 copy-start.3
  4.6 0.8 copy-start.4
  5.4 0.8 copy-start.5
  6.2 0.8 copy-start.6
  6.9 0.7 copy-start.7
  7.6 0.7 copy-start.8
  8.3 0.7 copy-start.9
  9.0 0.7 copy-start.10
  9.7 0.7 copy-start.11
  10.4 0.7 copy-start.12

commit v2 on v1

--- a/solution.py
+++ b/solution.py
@@ -185,47 +185,63 @@
     restrict2[...] = found
     prolong2[...] = inverse_order(order_rows, tiles2, 8)
 
+    @pl.when(b == 0)
+    def _():
+        incoming[:, 2] = jnp.zeros((incoming.shape[0], 8, LANES), jnp.float32)
+
+    @pl.when(b == spans - 1)
+    def _():
+        incoming[:, 3] = jnp.zeros((incoming.shape[0], 8, LANES), jnp.float32)
+
     pl.semaphore_wait(barrier, spans + 1)
 
     sends = []
 
     def copies_of(x):
         places = (
-            (1, (prev_a, b)),
-            (0, (next_a, b)),
-            (3, (a, prev_b)),
-            (2, (a, next_b)),
+            (1, (prev_a, b), None, None),
+            (0, (next_a, b), None, None),
+            (3, (a, prev_b), b > 0, b < spans - 1),
+            (2, (a, next_b), b < spans - 1, b > 0),
         )
         return [
-            pltpu.make_async_remote_copy(
-                src_ref=outgoing.at[x],
-                dst_ref=incoming.at[x, slot],
-                send_sem=send_sem.at[x, slot],
-                recv_sem=recv_sem.at[x, slot],
-                device_id=who,
-                device_id_type=MESH,
-            )
-            for slot, who in places
+            (
+                pltpu.make_async_remote_copy(
+                    src_ref=outgoing.at[x],
+                    dst_ref=incoming.at[x, slot],
+                    send_sem=send_sem.at[x, slot],
+                    recv_sem=recv_sem.at[x, slot],
+                    device_id=who,
+                    device_id_type=MESH,
+                ),
+                sends_it,
+                gets_it,
+            )
+            for slot, who, sends_it, gets_it in places
         ]
+
+    def when(condition, action):
+        if condition is None:
+            action()
+        else:
+            pl.when(condition)(action)
 
     def exchange_start(x, table, picks, tiles):
         places = picks[...]
         tables = [table[pl.ds(h, 8, stride=tiles), :] for h in range(tiles)]
         outgoing[x] = lookup(tables, places % LANES, places // LANES)
-        for copy in copies_of(x):
-            copy.start()
-            sends.append(copy)
+        for copy, sends_it, _ in copies_of(x):
+            when(sends_it, copy.start)
+            sends.append((sends_it, copy))
 
     def exchange_end(x):
-        for copy in copies_of(x):
-            copy.wait_recv()
+        for copy, _, gets_it in copies_of(x):
+            when(gets_it, copy.wait_recv)
         first_half = lane < HALF
-        block2 = jnp.where(b > 0, incoming[x, 2], 0.0)
-        block3 = jnp.where(b < spans - 1, incoming[x, 3], 0.0)
         halo[...] = jnp.where(
             row < 4,
             jnp.where(first_half, incoming[x, 0], incoming[x, 1]),
-            jnp.where(first_half, block2, block3),
+            jnp.where(first_half, incoming[x, 2], incoming[x, 3]),
         )
 
     def store_table(table, vector, tiles):
@@ -383,7 +399,7 @@
             )
         for copy in copies:
             copy.start()
-            sends.append(copy)
+            sends.append((None, copy))
         for copy in copies:
             copy.wait_recv()
         distance = lax.rem(b - high3 + spans, spans)
@@ -434,8 +450,8 @@
     solution_ref[...] = table1[pl.ds(0, 4 * tiles1), :]
     residual_ref[...] = right1[...] - operate1(x)
 
-    for copy in sends:
-        copy.wait_send()
+    for sends_it, copy in sends:
+        when(sends_it, copy.wait_send)
 
 
 def per_device(streams, spans, *arrays):
@@ -490,11 +506,11 @@
     results = pl.pallas_call(
         functools.partial(cycle_kernel, tiles1, tiles2, streams, spans),
         out_shape=(out, out),
-        in_specs=[pl.BlockSpec(memory_space=pl.ANY)] * len(arrays),
+        in_specs=[pl.BlockSpec(memory_space=pltpu.HBM)] * len(arrays),
         out_specs=[pl.BlockSpec(memory_space=pltpu.VMEM)] * 2,
         scratch_shapes=scratch,
         compiler_params=pltpu.CompilerParams(
-            collective_id=0, has_side_effects=True, vmem_limit_bytes=48 * 1024 * 1024
+            collective_id=0, has_side_effects=True, vmem_limit_bytes=67_000_000
         ),
         name="cycle",
     )(*arrays)

time: 92.5 us -> 80.3 us (0.87); the launches traced: 90.9 us -> 80.1 us
  local copies, waits for them, and re-layouts: 11.7 us -> 2.03 us
  Pallas kernels: 78.5 us -> 77.4 us
    unnamed x26 -> x2, local copies, waits for them, and re-layouts: 10.4 us -> 0.01 us
    pallas_call x1, Pallas kernels: 78.5 us -> 77.4 us  [per_device(): pl.pallas_call(functools.partial(cycle_kernel, tiles1, tiles2, streams, s...]
where the time goes in v2:
time: 80.3 us; the launch traced here: 80.1 us
  Pallas kernels  77.4 us (96%)
  local copies, waits for them, and re-layouts  2.03 us (3%)
    pallas_call x1, Pallas kernels, per_device(): pl.pallas_call(functools.partial(cycle_kernel, tiles1, tiles2, streams, s...  77.4 us
    reshape x2, local copies, waits for them, and re-layouts, per_device(): return tuple((r.reshape(4, rows1) for r in results))  2.02 us

profile of v2, /device:TPU:1, one launch (start us, length us, event | category | flops | bytes accessed | tf_op | source)
XLA Modules:
  0.0 80.1 jit_solution(2464108212187701467)
XLA Ops:
  0.6 77.4 %cycle.1 = (f32[64,128]{1,0:T(8,128)}, f32[64,128]{1,0:T(8,128)}) custom-call(f32[4,2048]{1,0:T(4,128)} %right_hbm.1, f32[8,4,4,2048]{3,2,1,0:T(4,128)} %values1_hbm.1, s32[8,2048]{1,0:T(8,128)} %columns1_hbm.1, s32[4,64]{1,0:T(4,128)} %sends1_hbm.1, s32[1,2048]{1,0:T(1,128)} %order1_hbm.1, f32[4,4,2048]{2,1,0:T(4,128)} %weights1_hbm.1, ...), custom_call_target="tpu_custom_call" | custom-call | tf_op jit(solution)/shard_map/cycle/pallas_call | solution.py:506
  78.0 0.0 copy-start
  78.0 1.4 %reshape.10 = f32[4,2048]{1,0:T(4,128)} reshape(f32[64,128]{1,0:T(8,128)} %get-tuple-element.4) | data formatting | bytes 65536 | tf_op jit(solution)/shard_map/reshape | solution.py:517
  79.4 0.0 copy-done
  79.4 0.6 reshape.11
Async XLA Ops:
  78.0 1.4 %copy-start = (f32[64,128]{1,0:T(8,128)S(1)}, f32[64,128]{1,0:T(8,128)}, u32[]{:S(2)}) copy-start(f32[64,128]{1,0:T(8,128)} %get-tuple-element.5) | copy-start | bytes 98308

commit v3 on v2

--- a/solution.py
+++ b/solution.py
@@ -25,6 +25,11 @@
         factors.append((rho_next * rho_prev, 2.0 * rho_next / CHEB_RADIUS))
         rho_prev = rho_next
     return factors
+
+
+def sorted_far(copies):
+    middle = len(copies) // 2
+    return [copies[n] for n in sorted(range(len(copies)), key=lambda n: abs(n - middle))]
 
 
 def gather_lanes(table, places):
@@ -56,7 +61,7 @@
     values2, columns2, picks2, restrict2, prolong2, weights2, inv2,
     order_rows, table1, table2, first1, first2, right2, part1, part2, product1, product2,
     outgoing, incoming, halo, gathered, group_own, group_all, table3, inv3,
-    in_sem, send_sem, recv_sem, group_send_sem, group_recv_sem,
+    in_sem, send_sem, recv_sem, group_send_sem, group_recv_sem, greet_sem,
 ):
     a = lax.axis_index("stream")
     b = lax.axis_index("span")
@@ -64,12 +69,8 @@
     prev_b, next_b = lax.rem(b + spans - 1, spans), lax.rem(b + 1, spans)
 
     barrier = pltpu.get_barrier_semaphore()
-    for who in (prev_a, next_a):
-        pl.semaphore_signal(barrier, inc=1, device_id=(who, b), device_id_type=MESH)
-    for step in range(1, spans):
-        pl.semaphore_signal(
-            barrier, inc=1, device_id=(a, lax.rem(b + step, spans)), device_id_type=MESH
-        )
+    for who in ((prev_a, b), (next_a, b), (a, prev_b), (a, next_b)):
+        pl.semaphore_signal(barrier, inc=1, device_id=who, device_id_type=MESH)
 
     loads = [
         pltpu.make_async_copy(src, dst, in_sem.at[n])
@@ -85,8 +86,8 @@
     ]
     for load in loads:
         load.start()
-    for load in loads:
-        load.wait()
+    for n in (0, 1, 3):
+        loads[n].wait()
 
     lane = lax.broadcasted_iota(jnp.int32, (8, LANES), 1)
     row = lax.broadcasted_iota(jnp.int32, (8, LANES), 0)
@@ -106,12 +107,19 @@
                     i, :, t * LANES : (t + 1) * LANES
                 ]
 
-    dense_blocks(values1_in, values1, tiles1)
     for t in range(tiles1):
         right1[pl.ds(t, 4, stride=tiles1), :] = right_in[:, t * LANES : (t + 1) * LANES]
-        columns1[pl.ds(t, 8, stride=tiles1), :] = columns1_in[:, t * LANES : (t + 1) * LANES]
-    for i in range(4):
-        inv1[pl.ds(i * tiles1, tiles1), :] = 1.0 / values1[pl.ds(i * 5 * tiles1, tiles1), :]
+        for i in range(4):
+            inv1[pl.ds(i * tiles1 + t, 1), :] = values1_in[
+                0, i, i : i + 1, t * LANES : (t + 1) * LANES
+            ]
+    inv1[...] = 1.0 / inv1[...]
+
+    def arrange_fine():
+        loads[2].wait()
+        dense_blocks(values1_in, values1, tiles1)
+        for t in range(tiles1):
+            columns1[pl.ds(t, 8, stride=tiles1), :] = columns1_in[:, t * LANES : (t + 1) * LANES]
 
     def pick_places(sends):
         stream_part = jnp.concatenate([sends[1:2, :], sends[0:1, :]], axis=1)
@@ -123,33 +131,6 @@
         )
 
     picks1[...] = pick_places(sends1_in)
-    picks2[...] = pick_places(sends2_in)
-
-    for i in range(4):
-        for k in range(8):
-            for t in range(tiles2):
-                values2[pl.ds(i * 32 * tiles2 + k * tiles2 + t, 4, stride=8 * tiles2), :] = (
-                    values2_in[k, i, :, t * LANES : (t + 1) * LANES]
-                )
-    for t in range(tiles2):
-        columns2[pl.ds(t, 8, stride=tiles2), :] = columns2_in[:, t * LANES : (t + 1) * LANES]
-    for i in range(4):
-        inv2[pl.ds(i * tiles2, tiles2), :] = 1.0 / values2[pl.ds(i * 5 * 8 * tiles2, tiles2), :]
-    dense_weights(weights1_in, weights1, tiles1)
-    dense_weights(weights2_in, weights2, tiles2)
-
-    quad = lane // 32
-    for t in range(tiles1):
-        order_rows[pl.ds(t, 1), :] = order1_in[:, t * LANES : (t + 1) * LANES]
-    for pair in range(2):
-        entry = row // 4 + 2 * pair
-        low = (lane * 4 + entry) % LANES
-        found = None
-        for q in range(4):
-            rows = order_rows[pl.ds(q, 4, stride=4), :]
-            taken = gather_lanes(jnp.concatenate([rows, rows], axis=0), low)
-            found = taken if found is None else jnp.where(quad == q, taken, found)
-        restrict1[pl.ds(pair * 8, 8), :] = found
 
     def inverse_order(rows_ref, count, tiles):
         total = jnp.zeros((2 * tiles, LANES), jnp.float32)
@@ -173,17 +154,52 @@
             )
         return (total[:tiles] + 32.0 * total[tiles:]).astype(jnp.int32)
 
-    prolong1[...] = inverse_order(order_rows, tiles1, tiles1)
-
-    for t in range(tiles2):
-        order_rows[pl.ds(t, 1), :] = order2_in[:, t * LANES : (t + 1) * LANES]
-    low = (lane * 4 + row % 4) % LANES
-    found = None
-    for q in range(4):
-        taken = gather_lanes(row_of(order_rows, q), low)
-        found = taken if found is None else jnp.where(quad == q, taken, found)
-    restrict2[...] = found
-    prolong2[...] = inverse_order(order_rows, tiles2, 8)
+    def arrange_middle():
+        for n in (5, 6, 7, 8, 10):
+            loads[n].wait()
+        picks2[...] = pick_places(sends2_in)
+        for i in range(4):
+            for k in range(8):
+                for t in range(tiles2):
+                    values2[pl.ds(i * 32 * tiles2 + k * tiles2 + t, 4, stride=8 * tiles2), :] = (
+                        values2_in[k, i, :, t * LANES : (t + 1) * LANES]
+                    )
+        for t in range(tiles2):
+            columns2[pl.ds(t, 8, stride=tiles2), :] = columns2_in[:, t * LANES : (t + 1) * LANES]
+        for i in range(4):
+            inv2[pl.ds(i * tiles2, tiles2), :] = 1.0 / values2[pl.ds(i * 5 * 8 * tiles2, tiles2), :]
+        dense_weights(weights1_in, weights1, tiles1)
+        dense_weights(weights2_in, weights2, tiles2)
+
+    def arrange_orders():
+        for n in (4, 9, 11, 12):
+            loads[n].wait()
+        quad = lane // 32
+        for t in range(tiles1):
+            order_rows[pl.ds(t, 1), :] = order1_in[:, t * LANES : (t + 1) * LANES]
+        for pair in range(2):
+            entry = row // 4 + 2 * pair
+            low = (lane * 4 + entry) % LANES
+            found = None
+            for q in range(4):
+                rows = order_rows[pl.ds(q, 4, stride=4), :]
+                taken = gather_lanes(jnp.concatenate([rows, rows], axis=0), low)
+                found = taken if found is None else jnp.where(quad == q, taken, found)
+            restrict1[pl.ds(pair * 8, 8), :] = found
+
+        prolong1[...] = inverse_order(order_rows, tiles1, tiles1)
+
+        for t in range(tiles2):
+            order_rows[pl.ds(t, 1), :] = order2_in[:, t * LANES : (t + 1) * LANES]
+        low = (lane * 4 + row % 4) % LANES
+        found = None
+        for q in range(4):
+            taken = gather_lanes(row_of(order_rows, q), low)
+            found = taken if found is None else jnp.where(quad == q, taken, found)
+        restrict2[...] = found
+        prolong2[...] = inverse_order(order_rows, tiles2, 8)
+
+    background = {0: arrange_fine, 1: arrange_middle, 2: arrange_orders}
 
     @pl.when(b == 0)
     def _():
@@ -193,8 +209,18 @@
     def _():
         incoming[:, 3] = jnp.zeros((incoming.shape[0], 8, LANES), jnp.float32)
 
-    pl.semaphore_wait(barrier, spans + 1)
-
+    pl.semaphore_wait(barrier, 4)
+
+    def greet(stage):
+        for step in (1 << stage, spans - (1 << stage)):
+            pl.semaphore_signal(
+                greet_sem.at[stage],
+                inc=1,
+                device_id=(a, lax.rem(b + step, spans)),
+                device_id_type=MESH,
+            )
+
+    stages = max((spans // 2 - 1).bit_length(), 0)
     sends = []
 
     def copies_of(x):
@@ -233,10 +259,14 @@
         for copy, sends_it, _ in copies_of(x):
             when(sends_it, copy.start)
             sends.append((sends_it, copy))
+        if x < stages:
+            greet(x)
 
     def exchange_end(x):
         for copy, _, gets_it in copies_of(x):
             when(gets_it, copy.wait_recv)
+        if x < stages:
+            pl.semaphore_wait(greet_sem.at[x], 2)
         first_half = lane < HALF
         halo[...] = jnp.where(
             row < 4,
@@ -250,6 +280,8 @@
 
     def operate1(x):
         exchange_start(x, table1, picks1, tiles1)
+        if x in background:
+            background[x]()
 
         def local(group, carry):
             where_to = columns1[pl.ds(pl.multiple_of(group * 8, 8), 8), :]
@@ -397,7 +429,7 @@
                     device_id_type=MESH,
                 )
             )
-        for copy in copies:
+        for copy in sorted_far(copies):
             copy.start()
             sends.append((None, copy))
         for copy in copies:
@@ -447,8 +479,11 @@
             table1[pl.ds(i * tiles1 + part * 8, 8), :] = total
             table1[pl.ds((4 + i) * tiles1 + part * 8, 8), :] = total
     x = smooth(operate1, table1, tiles1, right1, inv1, False, x)
-    solution_ref[...] = table1[pl.ds(0, 4 * tiles1), :]
-    residual_ref[...] = right1[...] - operate1(x)
+    for t in range(tiles1):
+        solution_ref[:, t * LANES : (t + 1) * LANES] = table1[pl.ds(t, 4, stride=tiles1), :]
+    part1[...] = right1[...] - operate1(x)
+    for t in range(tiles1):
+        residual_ref[:, t * LANES : (t + 1) * LANES] = part1[pl.ds(t, 4, stride=tiles1), :]
 
     for sends_it, copy in sends:
         when(sends_it, copy.wait_send)
@@ -501,9 +536,10 @@
         pltpu.SemaphoreType.DMA((exchanges, 4)),
         pltpu.SemaphoreType.DMA((KC - 1, spans)),
         pltpu.SemaphoreType.DMA((KC - 1, spans)),
+        pltpu.SemaphoreType.REGULAR((4,)),
     ]
-    out = jax.ShapeDtypeStruct((4 * tiles1, LANES), f32)
-    results = pl.pallas_call(
+    out = jax.ShapeDtypeStruct((4, rows1), f32)
+    return pl.pallas_call(
         functools.partial(cycle_kernel, tiles1, tiles2, streams, spans),
         out_shape=(out, out),
         in_specs=[pl.BlockSpec(memory_space=pltpu.HBM)] * len(arrays),
@@ -514,7 +550,6 @@
         ),
         name="cycle",
     )(*arrays)
-    return tuple(r.reshape(4, rows1) for r in results)
 
 
 def solution(mesh):

time: 80.3 us -> 79.2 us (0.986)
  Pallas kernels: 77.4 us -> 76.4 us
    reshape x2 -> x0, local copies, waits for them, and re-layouts: 2.02 us -> none  [per_device(): return tuple((r.reshape(4, rows1) for r in results))]
    unnamed x2 -> x4, local copies, waits for them, and re-layouts: 0.01 us -> 2 us
    pallas_call x1, Pallas kernels: 77.4 us -> 76.4 us  [per_device(): pl.pallas_call(functools.partial(cycle_kernel, tiles1, tiles2, streams, s...]
where the time goes in v3:
time: 79.2 us; the launch traced here: 79 us
  Pallas kernels  76.4 us (96%)
  local copies, waits for them, and re-layouts  2 us (3%)
    pallas_call x1, Pallas kernels, per_device(): pl.pallas_call(functools.partial(cycle_kernel, tiles1, tiles2, streams, s...  76.4 us
    unnamed x4, local copies, waits for them, and re-layouts  2 us

profile of v3, /device:TPU:1, one launch (start us, length us, event | category | flops | bytes accessed | tf_op | source)
XLA Modules:
  0.0 79.0 jit_solution(1628064689250292397)
XLA Ops:
  0.6 76.4 %cycle.1 = (f32[4,2048]{1,0:T(4,128)}, f32[4,2048]{1,0:T(4,128)}) custom-call(f32[4,2048]{1,0:T(4,128)} %right_hbm.1, f32[8,4,4,2048]{3,2,1,0:T(4,128)} %values1_hbm.1, s32[8,2048]{1,0:T(8,128)} %columns1_hbm.1, s32[4,64]{1,0:T(4,128)} %sends1_hbm.1, s32[1,2048]{1,0:T(1,128)} %order1_hbm.1, f32[4,4,2048]{2,1,0:T(4,128)} %weights1_hbm.1, ...), custom_call_target="tpu_custom_call" | custom-call | tf_op jit(solution)/shard_map/cycle/pallas_call | solution.py:542
  77.0 0.0 copy-start
  77.0 1.4 %copy.17 = f32[4,2048]{1,0:T(4,128)} copy(f32[4,2048]{1,0:T(4,128)} %get-tuple-element.4) | data formatting | bytes 65536
  78.4 0.0 copy-done
  78.4 0.6 copy.18
Async XLA Ops:
  77.0 1.4 %copy-start = (f32[4,2048]{1,0:T(4,128)S(1)}, f32[4,2048]{1,0:T(4,128)}, u32[]{:S(2)}) copy-start(f32[4,2048]{1,0:T(4,128)} %get-tuple-element.5) | copy-start | bytes 98308
